TPU v7x, 128 devices: a whole 4x4x4 slice. The times are simulated.
128 devices in a mesh: rcv: 8 (over x_hi, z), src: 16 (over y, x_lo, core).
Axes of the slice: x: 4 (x_hi: 2, x_lo: 2; x = x_hi * 2 + x_lo), y: 4, z: 4, core: 2. Of those that a mesh axis runs over, the one named last changes fastest.
Arguments:
- reflection: bfloat16 [2, 16384, 16384], P(None, 'rcv', 'src'), may hold values from -6 to 6
- green: bfloat16 [2, 16384, 512], P(None, 'rcv', 'src'), may hold values from -0.046875 to 0.046875
- tile_mask: int32 [64, 64], replicated, may hold values from 0 to 1, as said below
- reference_index: int32 [512], P(('rcv', 'src')), may hold values from 0 to 511
Outputs:
- aligned: float32 [512, 2, 512], P(('rcv', 'src'))
Inputs may be any that keep to these rules, and one draw needn't show every extreme that they name: `tile_mask`: entries below the diagonal are 0.
All inputs are finite; a program needn't handle non-finite values.
Results may differ from a plain program's by a relative error of at most 0.02.
Values may be sent and summed in bfloat16 or wider, within the bound.
No kernel may reach another device: no remote copies, remote signals or barrier semaphores. Data moves between devices by JAX's collectives and lax.ppermute only.
A program may use at most 128 MiB of HBM per device.

v0:
```python
import jax
import jax.numpy as jnp
from jax import lax
from jax.sharding import PartitionSpec as P

P_SIZE = 512
TILE = 256


def filled_up(lines, devices):
    spare = -lines.shape[0] % devices
    if not spare:
        return lines
    return jnp.concatenate([lines, jnp.zeros((spare, *lines.shape[1:]), lines.dtype)])


def spread(value, axis, root):
    lines = jnp.where(lax.axis_index(axis) == root, value, jnp.zeros_like(value)).reshape(
        -1, *value.shape[1:][-1:]
    )
    padded = filled_up(lines, lax.axis_size(axis))
    own = lax.psum_scatter(padded, axis, scatter_dimension=0, tiled=True)
    return lax.all_gather(own, axis, axis=0, tiled=True)[: len(lines)].reshape(value.shape)


def across(first, second, precision=None):
    return lax.dot_general(
        first,
        second,
        (((0,), (0,)), ((), ())),
        precision=precision,
        preferred_element_type=jnp.float32,
    )


def body(reflection, green, tile_mask, reference_index):
    rows_blk = reflection.shape[1]
    col_count = reflection.shape[2]
    rcv_index = lax.axis_index("rcv")
    src_index = lax.axis_index("src")
    green_block = lax.all_gather(green, "src", axis=2, tiled=True)
    src_per_rcv = lax.axis_size("src") // lax.axis_size("rcv")
    green_piece = lax.dynamic_slice_in_dim(
        green_block, src_index % src_per_rcv * col_count, col_count, 1
    )
    green_src = spread(green_piece, "rcv", src_index // src_per_rcv)
    row_tiles_count = rows_blk // TILE
    col_tiles_count = col_count // TILE
    tile_block = lax.dynamic_slice(
        tile_mask,
        (rcv_index * row_tiles_count, src_index * col_tiles_count),
        (row_tiles_count, col_tiles_count),
    )
    row_ids = rcv_index * row_tiles_count + jnp.arange(row_tiles_count)
    col_ids = src_index * col_tiles_count + jnp.arange(col_tiles_count)
    kept_tiles = tile_block == 1
    off_diag = kept_tiles & (row_ids[:, None] != col_ids[None, :])
    shaped = reflection.reshape(2, row_tiles_count, TILE, col_tiles_count, TILE)
    zero_value = jnp.zeros((), jnp.bfloat16)
    acquired = jnp.where(kept_tiles[None, :, None, :, None], shaped, zero_value).reshape(
        2, rows_blk, col_count
    )
    mirror_part = jnp.where(off_diag[None, :, None, :, None], shaped, zero_value).reshape(
        2, rows_blk, col_count
    )
    data_wide = jnp.concatenate([acquired[0], acquired[1], mirror_part[0], mirror_part[1]], axis=1)
    green_wide = jnp.concatenate([green_block[0], green_block[1]], axis=1)
    products = across(data_wide, green_wide)

    def quarter(row_slot, col_slot):
        return products[
            row_slot * col_count : (row_slot + 1) * col_count,
            col_slot * P_SIZE : (col_slot + 1) * P_SIZE,
        ]

    front_real = (quarter(0, 0) + quarter(1, 1)).astype(jnp.bfloat16)
    front_imag = (quarter(1, 0) - quarter(0, 1)).astype(jnp.bfloat16)
    back_real = (quarter(2, 0) - quarter(3, 1)).astype(jnp.bfloat16)
    back_imag = (quarter(3, 0) + quarter(2, 1)).astype(jnp.bfloat16)
    src_real = green_src[0]
    src_imag = green_src[1]
    green_stack = jnp.concatenate([src_real, src_imag], axis=0)
    mirror_left = jnp.concatenate(
        [
            jnp.concatenate([back_real, back_imag], axis=1),
            jnp.concatenate([back_imag, -back_real], axis=1),
        ],
        axis=0,
    )
    mirrored = across(green_stack, mirror_left)
    weights = jnp.concatenate(
        [
            jnp.concatenate([src_real, src_imag], axis=1),
            jnp.concatenate([-src_imag, src_real], axis=1),
        ],
        axis=0,
    )
    left_rows = jnp.concatenate([front_real, front_imag], axis=0)
    combined = across(left_rows, weights) + mirrored
    focal = lax.psum_scatter(combined, ("rcv", "src"), scatter_dimension=0, tiled=True)
    focal_real = focal[:, :P_SIZE]
    focal_imag = focal[:, P_SIZE:]
    chosen = jnp.arange(P_SIZE)[None, :] == reference_index[:, None]
    anchor_real = jnp.sum(jnp.where(chosen, focal_real, 0.0), axis=1)[:, None]
    anchor_imag = jnp.sum(jnp.where(chosen, focal_imag, 0.0), axis=1)[:, None]
    out_real = focal_real * anchor_real + focal_imag * anchor_imag
    out_imag = focal_imag * anchor_real - focal_real * anchor_imag
    return jnp.stack([out_real, out_imag], axis=1)


def solution(mesh):
    return jax.shard_map(
        body,
        mesh=mesh,
        in_specs=(P(None, "rcv", "src"), P(None, "rcv", "src"), P(), P(("rcv", "src"))),
        out_specs=P(("rcv", "src"), None, None),
        check_vma=False,
    )
```

profile of v0, /device:TPU:1, one launch (start us, length us, event | category | flops | bytes accessed | tf_op | source)
XLA Modules:
  0.0 371.1 jit_solution(2756795983004442803)
XLA Ops:
  6.5 0.0 all-gather.3.cloned.1.call-start
  6.5 1.9 copy.12
  8.5 0.0 all-gather.3.cloned.1.call-update
  8.5 0.0 reduce-scatter.2.cloned.1.call-start
  8.6 14.5 %reshape.34 = bf16[2,8,256,4,256]{4,3,2,1,0:T(4,128)(2,1)} reshape(bf16[2,2048,1024]{2,1,0:T(8,128)(2,1)} %param.4) | data formatting | bytes 16777216 | tf_op jit(solution)/shard_map/reshape | solution.py:58
  23.1 0.8 compare_and_fusion
  23.9 26.3 %all-gather.3.cloned.1.call-done = bf16[2,2048,512]{1,0,2:T(2,128)(2,1)} async-done(((bf16[2,2048,32]{1,0,2:T(2,128)(2,1)}), bf16[2,2048,512]{1,0,2:T(2,128)(2,1)}) %all-gather.3.cloned.1.call-update) | async-done | bytes 4194320 | tf_op jit(solution)/shard_map/all_gather | solution.py:41
  50.1 4.4 %constant_dynamic-slice_fusion = bf16[2,1024,512]{1,0,2:T(2,128)(2,1)} fusion(bf16[2,2048,512]{1,0,2:T(2,128)(2,1)} %all-gather.3.cloned.1.call-done, s32[]{:T(128)S(6)} %select_n.49), kind=kLoop, calls=%fused_computation.52 | loop fusion | bytes 4194308 | tf_op jit(solution)/shard_map/dynamic_slice | solution.py:43
  54.5 4.7 %copy.19 = bf16[2,1024,512]{2,1,0:T(8,128)(2,1)S(1)} copy(bf16[2,1024,512]{1,0,2:T(2,128)(2,1)} %constant_dynamic-slice_fusion) | data formatting | bytes 4194304
  59.2 1.5 broadcast_select_fusion.2
  60.7 0.0 reduce-scatter.2.cloned.1.call-update
  60.7 0.0 all-gather.5.cloned.1.call-start
  60.8 8.2 %broadcast_select_fusion.1 = (bf16[2,8,256,4,256]{4,3,2,1,0:T(4,128)(2,1)S(1)}, bf16[2,8,256,4,256]{4,3,2,1,0:T(4,128)(2,1)S(1)}) fusion(bf16[2,8,256,4,256]{4,3,2,1,0:T(4,128)(2,1)} %reshape.34, pred[8,4]{1,0:T(8,128)(4,1)S(1)} %get-tuple-element.10, pred[8,4]{1,0:T(8,128)(4,1)S(1)} %get-tuple-element.9), kind=kLoop, calls=%fused_computation.9 | loop fusion | flops 8388608 | bytes 25165888 | tf_op jit(solution)/shard_map/jit(_where)/select_n | solution.py:60
  68.9 6.2 %fusion.42 = (bf16[1,8,256,4,256]{4,3,2,1,0:T(4,128)(2,1)S(1)}, bf16[1,8,256,4,256]{4,3,2,1,0:T(4,128)(2,1)S(1)}, bf16[1,8,256,4,256]{4,3,2,1,0:T(4,128)(2,1)S(1)}, bf16[1,8,256,4,256]{4,3,2,1,0:T(4,128)(2,1)S(1)}) fusion(bf16[2,8,256,4,256]{4,3,2,1,0:T(4,128)(2,1)S(1)} %get-tuple-element.16, bf16[2,8,256,4,256]{4,3,2,1,0:T(4,128)(2,1)S(1)} %get-tuple-element.17), kind=kLoop, calls=%fused_computation.58 | loop fusion | bytes 33554432 | tf_op jit(solution)/shard_map/slice | solution.py:66
  75.1 3.0 copy.21
  78.1 3.0 copy.22
  81.1 3.0 copy.23
  84.1 0.0 copy-start
  84.1 3.0 copy.20
  87.1 0.0 copy-done
  87.1 6.9 %fusion.44 = (bf16[1,2048,512]{1,0,2:T(2,128)(2,1)}, bf16[1,2048,512]{1,0,2:T(2,128)(2,1)}) fusion(bf16[2,2048,512]{1,0,2:T(2,128)(2,1)S(1)} %copy-done), kind=kLoop, calls=%fused_computation.60 | loop fusion | bytes 8388608 | tf_op jit(solution)/shard_map/slice | solution.py:67
  94.1 9.0 %copy.17 = bf16[1,2048,512]{2,1,0:T(8,128)(2,1)S(1)} copy(bf16[1,2048,512]{1,0,2:T(2,128)(2,1)} %get-tuple-element.20) | data formatting | bytes 4194304
  103.0 10.5 %copy.18 = bf16[1,2048,512]{2,1,0:T(8,128)(2,1)} copy(bf16[1,2048,512]{1,0,2:T(2,128)(2,1)} %get-tuple-element.21) | data formatting | bytes 4194304
  113.5 20.8 %reduce-scatter.2.cloned.1.call-done = bf16[256,512]{1,0:T(8,128)(2,1)} async-done(((bf16[2048,512]{1,0:T(8,128)(2,1)}), bf16[256,512]{1,0:T(8,128)(2,1)}) %reduce-scatter.2.cloned.1.call-update) | async-done | bytes 262160 | tf_op jit(solution)/shard_map/reduce_scatter | solution.py:22
  134.4 0.0 all-gather.5.cloned.1.call-update
  134.4 0.2 all-reduce.3.cloned.1.call-start
  134.6 27.2 %fusion = f32[4096,1024]{0,1:T(8,128)} fusion(bf16[2048,1024]{1,0:T(8,128)(2,1)} %bitcast.27, bf16[2048,1024]{1,0:T(8,128)(2,1)} %bitcast.26, bf16[2048,1024]{1,0:T(8,128)(2,1)} %bitcast.25, bf16[2048,1024]{1,0:T(8,128)(2,1)} %bitcast.28, bf16[2048,512]{1,0:T(8,128)(2,1)} %bitcast.30, bf16[2048,512]{1,0:T(8,128)(2,1)S(1)} %bitcast.29), kind=kOutput, calls=%fused_computation | convolution fusion | flops 17255366656 | bytes 37748736 | tf_op jit(solution)/shard_map/dot_general | solution.py:27
  161.8 2.8 fusion.40
  164.6 7.2 %fusion.27 = (bf16[1024,512]{0,1:T(8,128)(2,1)S(1)}, bf16[1024,512]{0,1:T(8,128)(2,1)}, bf16[1024,512]{0,1:T(8,128)(2,1)}) fusion(f32[4096,1024]{0,1:T(8,128)} %fusion), kind=kLoop, calls=%fused_computation.30 | loop fusion | flops 3145728 | bytes 15728640 | tf_op jit(solution)/shard_map/convert_element_type | solution.py:79
  171.8 18.9 %all-gather.5.cloned.1.call-done = bf16[2048,512]{1,0:T(8,128)(2,1)} async-done(((bf16[256,512]{1,0:T(8,128)(2,1)}), bf16[2048,512]{1,0:T(8,128)(2,1)}) %all-gather.5.cloned.1.call-update) | async-done | bytes 2097168 | tf_op jit(solution)/shard_map/all_gather | solution.py:23
  190.7 0.0 copy-start.2
  190.7 0.0 copy-start.3
  190.7 1.9 fusion.45
  192.6 0.0 copy-done.2
  192.6 0.3 copy-done.3
  192.8 0.0 copy-start.1
  192.8 2.4 fusion.11
  195.2 0.0 copy-done.1
  195.2 0.0 copy-start.4
  195.2 18.3 %fusion.34 = f32[512,1024]{1,0:T(8,128)} fusion(f32[512,1024]{1,0:T(8,128)S(1)} %fusion.11, bf16[2048,512]{1,0:T(8,128)(2,1)S(1)} %copy-done.1, bf16[1024,512]{0,1:T(8,128)(2,1)S(1)} %get-tuple-element.7, bf16[1024,512]{0,1:T(8,128)(2,1)S(1)} %get-tuple-element.11, bf16[1024,512]{0,1:T(8,128)(2,1)S(1)} %get-tuple-element.8), kind=kOutput, calls=%fused_computation.41 | convolution fusion | flops 2164785152 | bytes 9437184 | tf_op jit(solution)/shard_map/dot_general | solution.py:27
  213.5 0.0 all-reduce.3.cloned.1.call-update
  213.5 148.7 %all-reduce.3.cloned.1.call-done = f32[512,1024]{1,0:T(8,128)} async-done(((f32[512,1024]{1,0:T(8,128)}), f32[512,1024]{1,0:T(8,128)}) %all-reduce.3.cloned.1.call-update) | async-done | bytes 2097168
  362.2 0.0 copy-done.4
  362.2 1.0 select_reduce_fusion.1
  363.1 0.8 add_bitcast_fusion
  364.0 0.6 copy.16
  (3 shorter events, 0.0 us)
Async XLA Ops:
  6.5 43.6 %all-gather.3.cloned.1.call-start = ((), (), s32[]{:S(2)}) async-start(), calls=%async_computation.1 | async-start | bytes 4456448 | tf_op jit(solution)/shard_map/all_gather | solution.py:41
  8.5 125.9 %reduce-scatter.2.cloned.1.call-start = ((), (), s32[]{:S(2)}) async-start(), calls=%async_computation.2 | async-start | bytes 2359296 | tf_op jit(solution)/shard_map/reduce_scatter | solution.py:22
  60.7 130.0 %all-gather.5.cloned.1.call-start = ((), (), s32[]{:S(2)}) async-start(), calls=%async_computation.3 | async-start | bytes 2359296 | tf_op jit(solution)/shard_map/all_gather | solution.py:23
  84.1 3.0 copy-start
  134.4 227.8 %all-reduce.3.cloned.1.call-start = ((), (), s32[]{:S(2)}) async-start(), calls=%async_computation.4 | async-start | bytes 4194304
  190.7 1.9 copy-start.2
  190.7 2.2 copy-start.3
  192.8 2.4 copy-start.1
  195.2 167.0 %copy-start.4 = (s32[4]{0:T(128)S(1)}, s32[4]{0:T(128)}, u32[]{:S(2)}) copy-start(s32[4]{0:T(128)} %param.7) | copy-start | bytes 52
Sparse Core Ops, SparseCore 0:
  9.1 41.0 all-gather.2
  60.8 73.5 reduce-scatter.1
  136.7 53.8 all-gather.4
  213.6 148.4 all-reduce.2
where the time goes:
time: 372 us; the launch traced here: 371 us
  waiting for transfers between devices  215 us (58%)
  local copies, waits for them, and re-layouts  71 us (19%)
  matrix products  47.8 us (13%)
  other arithmetic  24 us (6%)
  between operations  13.2 us (4%)
    unnamed x5, waiting for transfers between devices  149 us
    dot_general x3, matrix products, across(): lax.dot_general(first, second, (((0,), (0,)), ((), ())), precision=precis...  47.8 us
    unnamed x18, local copies, waits for them, and re-layouts  38.4 us
    all_gather x1, waiting for transfers between devices, body(): green_block = lax.all_gather(green, 'src', axis=2, tiled=True)  26.3 us
    reduce_scatter x1, waiting for transfers between devices, spread(): own = lax.psum_scatter(padded, axis, scatter_dimension=0, tiled=True)  20.8 us
    all_gather x1, waiting for transfers between devices, spread(): lax.all_gather(own, axis, axis=0, tiled=True)[:len(lines)]  18.9 us
    reshape x1, local copies, waits for them, and re-layouts, body(): shaped = reflection.reshape(2, row_tiles_count, TILE, col_tiles_count, TILE)  14.5 us
    select_n x1, other arithmetic, body(): jnp.where(kept_tiles[None, :, None, :, None], shaped, zero_value)  8.16 us
  transfers between devices with their start and end apart: 4, of which 4 were waited for; matrix products, arithmetic and copies ran while one was open for 28% of the time, Pallas kernels for 0%

commit v1 on v0

--- a/solution.py
+++ b/solution.py
@@ -20,7 +20,9 @@
     )
     padded = filled_up(lines, lax.axis_size(axis))
     own = lax.psum_scatter(padded, axis, scatter_dimension=0, tiled=True)
-    return lax.all_gather(own, axis, axis=0, tiled=True)[: len(lines)].reshape(value.shape)
+    return jnp.concatenate(
+        lax.all_to_all(jnp.stack([own] * lax.axis_size(axis)), axis, 0, 0), axis=0
+    )[: len(lines)].reshape(value.shape)
 
 
 def across(first, second, precision=None):

time: 372 us -> 351 us (0.944)
  waiting for transfers between devices: 215 us -> 199 us
  matrix products: 47.8 us -> 33.8 us
  local copies, waits for them, and re-layouts: 71 us -> 76.1 us
  starting transfers between devices: 0.3 us -> 4.05 us
    all_gather x1 -> x0, waiting for transfers between devices: 18.9 us -> none  [spread(): lax.all_gather(own, axis, axis=0, tiled=True)[:len(lines)]]
    dot_general x3, matrix products: 47.8 us -> 33.8 us  [across(): lax.dot_general(first, second, (((0,), (0,)), ((), ())), precision=precis...]
    unnamed x5 -> x4, waiting for transfers between devices: 149 us -> 154 us
    all_to_all x0 -> x1, starting transfers between devices: none -> 3.78 us  [spread(): lax.all_to_all(jnp.stack([own] * lax.axis_size(axis)), axis, 0, 0)]
    unnamed x18 -> x20, local copies, waits for them, and re-layouts: 38.4 us -> 40.9 us
  transfers between devices with their start and end apart: 4 -> 4, of which waited for: 4 -> 3; matrix products, arithmetic and copies ran while one was open for 28% -> 31% of each run, Pallas kernels for 0% -> 0%
where the time goes in v1:
time: 351 us; the launch traced here: 350 us
  waiting for transfers between devices  199 us (57%)
  local copies, waits for them, and re-layouts  76.1 us (22%)
  matrix products  33.8 us (10%)
  other arithmetic  23.1 us (7%)
  between operations  13.2 us (4%)
  starting transfers between devices  4.05 us (1%)
    unnamed x4, waiting for transfers between devices  154 us
    unnamed x20, local copies, waits for them, and re-layouts  40.9 us
    dot_general x3, matrix products, across(): lax.dot_general(first, second, (((0,), (0,)), ((), ())), precision=precis...  33.8 us
    all_gather x1, waiting for transfers between devices, body(): green_block = lax.all_gather(green, 'src', axis=2, tiled=True)  26.5 us
    reduce_scatter x1, waiting for transfers between devices, spread(): own = lax.psum_scatter(padded, axis, scatter_dimension=0, tiled=True)  19.1 us
    reshape x1, local copies, waits for them, and re-layouts, body(): shaped = reflection.reshape(2, row_tiles_count, TILE, col_tiles_count, TILE)  14.5 us
    select_n x1, other arithmetic, body(): jnp.where(kept_tiles[None, :, None, :, None], shaped, zero_value)  8.16 us
    convert_element_type x1, other arithmetic, body(): back_imag = (quarter(3, 0) + quarter(2, 1)).astype(jnp.bfloat16)  7.06 us
  transfers between devices with their start and end apart: 4, of which 3 were waited for; matrix products, arithmetic and copies ran while one was open for 31% of the time, Pallas kernels for 0%

profile of v1, /device:TPU:1, one launch (start us, length us, event | category | flops | bytes accessed | tf_op | source)
XLA Modules:
  0.0 349.8 jit_solution(15656305368218575176)
XLA Ops:
  6.5 0.0 all-gather.2.cloned.1.call-start
  6.5 1.9 copy.12
  8.5 0.0 all-gather.2.cloned.1.call-update
  8.5 0.0 reduce-scatter.2.cloned.1.call-start
  8.6 14.5 %reshape.35 = bf16[2,8,256,4,256]{4,3,2,1,0:T(4,128)(2,1)} reshape(bf16[2,2048,1024]{2,1,0:T(8,128)(2,1)} %param.4) | data formatting | bytes 16777216 | tf_op jit(solution)/shard_map/reshape | solution.py:60
  23.1 0.8 compare_and_fusion
  23.9 26.5 %all-gather.2.cloned.1.call-done = bf16[2,2048,512]{1,0,2:T(2,128)(2,1)} async-done(((bf16[2,2048,32]{1,0,2:T(2,128)(2,1)}), bf16[2,2048,512]{1,0,2:T(2,128)(2,1)}) %all-gather.2.cloned.1.call-update) | async-done | bytes 4194320 | tf_op jit(solution)/shard_map/all_gather | solution.py:43
  50.3 4.4 %constant_dynamic-slice_fusion = bf16[2,1024,512]{1,0,2:T(2,128)(2,1)} fusion(bf16[2,2048,512]{1,0,2:T(2,128)(2,1)} %all-gather.2.cloned.1.call-done, s32[]{:T(128)S(6)} %select_n.49), kind=kLoop, calls=%fused_computation.55 | loop fusion | bytes 4194308 | tf_op jit(solution)/shard_map/dynamic_slice | solution.py:45
  54.7 4.7 %copy.19 = bf16[2,1024,512]{2,1,0:T(8,128)(2,1)S(1)} copy(bf16[2,1024,512]{1,0,2:T(2,128)(2,1)} %constant_dynamic-slice_fusion) | data formatting | bytes 4194304
  59.4 1.5 broadcast_select_fusion.2
  60.9 0.0 reduce-scatter.2.cloned.1.call-update
  60.9 8.2 %broadcast_select_fusion.1 = (bf16[2,8,256,4,256]{4,3,2,1,0:T(4,128)(2,1)S(1)}, bf16[2,8,256,4,256]{4,3,2,1,0:T(4,128)(2,1)S(1)}) fusion(bf16[2,8,256,4,256]{4,3,2,1,0:T(4,128)(2,1)} %reshape.35, pred[8,4]{1,0:T(8,128)(4,1)S(1)} %get-tuple-element.10, pred[8,4]{1,0:T(8,128)(4,1)S(1)} %get-tuple-element.9), kind=kLoop, calls=%fused_computation.9 | loop fusion | flops 8388608 | bytes 25165888 | tf_op jit(solution)/shard_map/jit(_where)/select_n | solution.py:62
  69.1 6.2 %fusion.47 = (bf16[1,8,256,4,256]{4,3,2,1,0:T(4,128)(2,1)S(1)}, bf16[1,8,256,4,256]{4,3,2,1,0:T(4,128)(2,1)S(1)}, bf16[1,8,256,4,256]{4,3,2,1,0:T(4,128)(2,1)S(1)}, bf16[1,8,256,4,256]{4,3,2,1,0:T(4,128)(2,1)S(1)}) fusion(bf16[2,8,256,4,256]{4,3,2,1,0:T(4,128)(2,1)S(1)} %get-tuple-element.16, bf16[2,8,256,4,256]{4,3,2,1,0:T(4,128)(2,1)S(1)} %get-tuple-element.17), kind=kLoop, calls=%fused_computation.61 | loop fusion | bytes 33554432 | tf_op jit(solution)/shard_map/slice | solution.py:68
  75.3 3.0 copy.23
  78.3 3.0 copy.22
  81.3 3.0 copy.21
  84.3 0.0 copy-start
  84.3 3.0 copy.20
  87.3 0.0 copy-done
  87.3 7.0 %fusion.49 = (bf16[1,2048,512]{1,0,2:T(2,128)(2,1)}, bf16[1,2048,512]{1,0,2:T(2,128)(2,1)}) fusion(bf16[2,2048,512]{1,0,2:T(2,128)(2,1)S(1)} %copy-done), kind=kLoop, calls=%fused_computation.63 | loop fusion | bytes 8388608 | tf_op jit(solution)/shard_map/slice | solution.py:69
  94.2 10.5 %copy.18 = bf16[1,2048,512]{2,1,0:T(8,128)(2,1)} copy(bf16[1,2048,512]{1,0,2:T(2,128)(2,1)} %get-tuple-element.21) | data formatting | bytes 4194304
  104.7 10.5 %copy.17 = bf16[1,2048,512]{2,1,0:T(8,128)(2,1)} copy(bf16[1,2048,512]{1,0,2:T(2,128)(2,1)} %get-tuple-element.20) | data formatting | bytes 4194304
  115.2 19.1 %reduce-scatter.2.cloned.1.call-done = bf16[256,512]{1,0:T(8,128)(2,1)} async-done(((bf16[2048,512]{1,0:T(8,128)(2,1)}), bf16[256,512]{1,0:T(8,128)(2,1)}) %reduce-scatter.2.cloned.1.call-update) | async-done | bytes 262160 | tf_op jit(solution)/shard_map/reduce_scatter | solution.py:22
  134.3 2.4 stack.8
  136.8 3.8 %all-to-all-start = ((bf16[8,256,512]{2,1,0:T(8,128)(2,1)}), bf16[8,256,512]{2,1,0:T(8,128)(2,1)S(1)}, u32[]{:S(2)}, u32[]{:S(2)}) async-start(bf16[8,256,512]{2,1,0:T(8,128)(2,1)} %stack.8), calls=%async_computation.1 | async-start | bytes 4194304 | tf_op jit(solution)/shard_map/all_to_all | solution.py:24
  140.6 0.2 all-reduce.3.cloned.1.call-start
  140.8 27.8 %fusion = f32[4096,1024]{0,1:T(8,128)} fusion(bf16[2048,1024]{1,0:T(8,128)(2,1)} %bitcast.27, bf16[2048,1024]{1,0:T(8,128)(2,1)} %bitcast.28, bf16[2048,1024]{1,0:T(8,128)(2,1)} %bitcast.29, bf16[2048,1024]{1,0:T(8,128)(2,1)} %bitcast.30, bf16[2048,512]{1,0:T(8,128)(2,1)} %bitcast.33, bf16[2048,512]{1,0:T(8,128)(2,1)} %bitcast.34), kind=kOutput, calls=%fused_computation | convolution fusion | flops 17255366656 | bytes 37748736 | tf_op jit(solution)/shard_map/dot_general | solution.py:29
  168.6 3.8 %fusion.45 = (bf16[1024,512]{0,1:T(8,128)(2,1)S(1)}, bf16[1024,512]{0,1:T(8,128)(2,1)}) fusion(f32[4096,1024]{0,1:T(8,128)} %fusion), kind=kLoop, calls=%fused_computation.60 | loop fusion | flops 1572864 | bytes 6291456 | tf_op jit(solution)/shard_map/neg | solution.py:88
  172.3 7.1 %fusion.27 = (bf16[1024,512]{0,1:T(8,128)(2,1)}, bf16[1024,512]{0,1:T(8,128)(2,1)}, bf16[1024,512]{0,1:T(8,128)(2,1)}) fusion(f32[4096,1024]{0,1:T(8,128)} %fusion), kind=kLoop, calls=%fused_computation.30 | loop fusion | flops 3145728 | bytes 15728640 | tf_op jit(solution)/shard_map/convert_element_type | solution.py:81
  179.4 0.0 all-to-all-done
  179.4 0.0 copy-start.3
  179.4 0.0 copy-start.4
  179.4 0.1 fusion.50
  179.6 0.1 bitcast_negate_fusion
  179.7 0.9 copy-done.3
  180.6 0.3 copy-done.4
  180.9 0.0 copy-start.1
  181.0 2.3 fusion.11
  183.3 0.0 copy-done.1
  183.3 0.0 copy-done.2
  183.3 0.0 copy-start.5
  183.3 3.7 %fusion.37 = f32[512,1024]{1,0:T(8,128)} fusion(f32[512,1024]{1,0:T(8,128)S(1)} %fusion.11, bf16[1024,512]{0,1:T(8,128)(2,1)S(1)} %get-tuple-element.7, bf16[1024,512]{0,1:T(8,128)(2,1)S(1)} %copy-done.2, bf16[1024,512]{0,1:T(8,128)(2,1)S(1)} %copy-done.1, bf16[1024,512]{1,0:T(8,128)(2,1)S(1)} %bitcast.32, bf16[1024,512]{1,0:T(8,128)(2,1)S(1)} %bitcast.36), kind=kOutput, calls=%fused_computation.44 | convolution fusion | flops 2168979456 | bytes 9437184 | tf_op jit(solution)/shard_map/dot_general | solution.py:29
  187.0 0.0 all-reduce.3.cloned.1.call-update
  187.1 153.8 %all-reduce.3.cloned.1.call-done = f32[512,1024]{1,0:T(8,128)} async-done(((f32[512,1024]{1,0:T(8,128)}), f32[512,1024]{1,0:T(8,128)}) %all-reduce.3.cloned.1.call-update) | async-done | bytes 2097168
  340.9 0.0 copy-done.5
  340.9 1.0 select_reduce_fusion.1
  341.9 0.8 add_bitcast_fusion
  342.7 0.6 copy.16
  (4 shorter events, 0.0 us)
Async XLA Ops:
  6.5 43.8 %all-gather.2.cloned.1.call-start = ((), (), s32[]{:S(2)}) async-start(), calls=%async_computation.2 | async-start | bytes 4456448 | tf_op jit(solution)/shard_map/all_gather | solution.py:43
  8.5 125.8 %reduce-scatter.2.cloned.1.call-start = ((), (), s32[]{:S(2)}) async-start(), calls=%async_computation.3 | async-start | bytes 2359296 | tf_op jit(solution)/shard_map/reduce_scatter | solution.py:22
  84.3 3.0 copy-start
  136.8 42.6 %all-to-all-start = ((bf16[8,256,512]{2,1,0:T(8,128)(2,1)}), bf16[8,256,512]{2,1,0:T(8,128)(2,1)S(1)}, u32[]{:S(2)}, u32[]{:S(2)}) async-start(bf16[8,256,512]{2,1,0:T(8,128)(2,1)} %stack.8), calls=%async_computation.1 | async-start | bytes 4194304 | tf_op jit(solution)/shard_map/all_to_all | solution.py:24
  140.6 200.3 %all-reduce.3.cloned.1.call-start = ((), (), s32[]{:S(2)}) async-start(), calls=%async_computation.4 | async-start | bytes 4194304
  179.4 1.2 copy-start.3
  179.4 1.5 copy-start.4
  180.9 2.3 copy-start.1
  181.0 2.4 copy-start.2
  183.3 157.6 %copy-start.5 = (s32[4]{0:T(128)S(1)}, s32[4]{0:T(128)}, u32[]{:S(2)}) copy-start(s32[4]{0:T(128)} %param.7) | copy-start | bytes 52
Sparse Core Ops, SparseCore 0:
  9.1 41.2 all-gather.1
  61.0 73.2 reduce-scatter.1
  187.2 153.6 all-reduce.2
